TPU v7x, 32 devices: a whole 2x2x4 slice. The times are simulated.
32 devices in a mesh: group: 2 (over x), replica: 16 (over z, y, core).
Axes of the slice: x: 2, y: 2, z: 4, core: 2. Of those that a mesh axis runs over, the one named last changes fastest.
Arguments:
- block_in: bfloat16 [16, 1024, 1024], P('replica', 'group'), may hold values from -6 to 6
- attn_gain: bfloat16 [1024], P('group'), may hold values from 0.5 to 1.5
- query_weight: bfloat16 [1024, 1024], P('group'), may hold values from -0.25 to 0.25
- key_weight: bfloat16 [1024, 512], P('group'), may hold values from -0.25 to 0.25
- value_weight: bfloat16 [1024, 512], P('group'), may hold values from -0.1875 to 0.1875
- out_weight: bfloat16 [1024, 1024], P('group'), may hold values from -1.5 to 1.5
- ffn_gain: bfloat16 [1024], P('group'), may hold values from 0.5 to 1.5
- router_weight: bfloat16 [1024, 16], P('group'), may hold values from -0.09375 to 0.09375
- expert_in: bfloat16 [16, 1024, 1024], P('group'), may hold values from -0.1875 to 0.1875
- expert_out: bfloat16 [16, 1024, 512], P('group'), may hold values from -1.5 to 1.5
- routes: int32 [16, 1024, 8], P('replica', 'group'), may hold values from 0 to 15, all different within a row; in each aligned block of 512 rows (0 to 511, 512 to 1023, ..., all dimensions but the last counted through in order) at most 384 rows name the same one
- prefix: int32 [16], P('replica'), may hold values from 102 to 512, as said below
- cotangent: bfloat16 [16, 1024, 1024], P('replica', 'group'), may hold values from -6 to 6
Outputs:
- block_out: bfloat16 [16, 1024, 1024], P('replica', 'group')
- input_grad: float32 [16, 1024, 1024], P('replica', 'group')
- attn_gain_grad: float32 [1024], P(('group', 'replica'))
- query_grad: float32 [1024, 1024], P(('group', 'replica'))
- key_grad: float32 [1024, 512], P(('group', 'replica'))
- value_grad: float32 [1024, 512], P(('group', 'replica'))
- out_grad: float32 [1024, 1024], P(None, ('group', 'replica'))
- ffn_gain_grad: float32 [1024], P(('group', 'replica'))
- router_grad: float32 [1024, 16], P(('group', 'replica'))
- expert_in_grad: float32 [16, 1024, 1024], P(None, ('group', 'replica'))
- expert_out_grad: float32 [16, 1024, 512], P(None, ('group', 'replica'))
Inputs may be any that keep to these rules, and one draw needn't show every extreme that they name: `routes`: each token names 8 different experts. Among the 512 tokens of one sequence block no expert is named more than 384 times, and in every draw some expert is named exactly 384 times by some block. Some sequence has a prefix of exactly 512.
All inputs are finite; a program needn't handle non-finite values.
Results may differ from a plain program's by a relative error of at most 0.017.
The roundings to bfloat16 on the way count: a program that leaves them out, or rounds other values in their place, can miss the bound.
Values may be sent and summed in bfloat16 or wider, within the bound.
No kernel may reach another device: no remote copies, remote signals or barrier semaphores. Data moves between devices by JAX's collectives and lax.ppermute only.
A program may use at most 448 MiB of HBM per device.

v0:
```python
import math
import jax
import jax.numpy as jnp
from jax import lax
from jax.sharding import PartitionSpec as P

HEADS = 16
KV_HEADS = 8
HEAD = 64
FF = 512
TOP = 8
EXPERTS = 16
CAP = 384
EPSILON = 1e-06
THETA_BASE = 10000.0
MASKED = -1e30
HIGHEST = lax.Precision.HIGHEST


def from_behind(value, axis, steps):
    count = lax.axis_size(axis)
    first, last = (max(0, -steps), min(count, count - steps))
    return lax.ppermute(value, axis, [(source, source + steps) for source in range(first, last)])


def normalize(values, gain):
    return values * lax.rsqrt(jnp.mean(values * values, -1, keepdims=True) + EPSILON) * gain


def rope_tables(positions, head_size):
    half_head = head_size // 2
    frequency = THETA_BASE ** (-jnp.arange(half_head, dtype=jnp.float32) * 2.0 / head_size)
    angles = positions.astype(jnp.float32)[:, None] * frequency[None, :]
    return (jnp.cos(angles)[:, None, :], jnp.sin(angles)[:, None, :])


def rotate(values, cosine, sine_table):
    half_head = values.shape[-1] // 2
    first_half = values[..., :half_head]
    second_half = values[..., half_head:]
    return jnp.concatenate(
        [
            first_half * cosine - second_half * sine_table,
            second_half * cosine + first_half * sine_table,
        ],
        -1,
    )


def rotate_back(gradient, cosine, sine_table):
    half_head = gradient.shape[-1] // 2
    first_half = gradient[..., :half_head]
    second_half = gradient[..., half_head:]
    return jnp.concatenate(
        [
            first_half * cosine + second_half * sine_table,
            second_half * cosine - first_half * sine_table,
        ],
        -1,
    )


def contract_rows(left, right):
    return lax.dot_general(
        left, right, (((0,), (0,)), ((), ())), preferred_element_type=jnp.float32
    )


def contract_cols(left, right):
    return lax.dot_general(
        left, right, (((1,), (1,)), ((), ())), preferred_element_type=jnp.float32
    )


def expert_forward(rows, weight_in, weight_out):
    gate_up = jnp.einsum("ecd,edf->ecf", rows, weight_in, preferred_element_type=jnp.float32)
    hidden = (jax.nn.silu(gate_up[..., :FF]) * gate_up[..., FF:]).astype(jnp.bfloat16)
    outputs = jnp.einsum("ecf,edf->ecd", hidden, weight_out, preferred_element_type=jnp.float32)
    return (gate_up, hidden, outputs)


def expert_backward(rows, gate_up, hidden, grad_rows, weight_in, weight_out):
    grad_hidden = jnp.einsum(
        "ecd,edf->ecf", grad_rows, weight_out, preferred_element_type=jnp.float32
    )
    grad_out_weight = jnp.einsum(
        "ecd,ecf->edf", grad_rows, hidden, preferred_element_type=jnp.float32
    )
    gate_part = gate_up[..., :FF]
    up_part = gate_up[..., FF:]
    sigmoid = jax.nn.sigmoid(gate_part)
    grad_gate = grad_hidden * up_part * sigmoid * (1.0 + gate_part * (1.0 - sigmoid))
    grad_up = grad_hidden * (gate_part * sigmoid)
    grad_gate_up = jnp.concatenate([grad_gate, grad_up], -1).astype(jnp.bfloat16)
    grad_in_weight = jnp.einsum(
        "ecd,ecf->edf", rows, grad_gate_up, preferred_element_type=jnp.float32
    )
    grad_rows_in = jnp.einsum(
        "ecf,edf->ecd", grad_gate_up, weight_in, preferred_element_type=jnp.float32
    )
    return (grad_rows_in, grad_in_weight, grad_out_weight)


def on_device(
    block_in,
    attn_gain,
    query_weight,
    key_weight,
    value_weight,
    out_weight,
    ffn_gain,
    router_weight,
    expert_in,
    expert_out,
    routes,
    prefix,
    cotangent,
):
    tokens = block_in.shape[1]
    width = block_in.shape[2]
    half_index = lax.axis_index("group")
    inputs = block_in[0].astype(jnp.float32)
    token_routes = routes[0]
    prefix_len = prefix[0]
    grad_out = cotangent[0].astype(jnp.float32)
    groups = HEADS // KV_HEADS
    score_scale = 1.0 / math.sqrt(HEAD)
    rows_block = min(tokens, 512)
    block_count = tokens // rows_block
    positions = half_index * tokens + jnp.arange(tokens, dtype=jnp.int32)
    key_positions = jnp.concatenate([positions - tokens, positions])
    cosine, sine_table = rope_tables(positions, HEAD)
    gain_attn, weight_q, weight_k, weight_v, weight_o = (
        lax.all_gather(attn_gain, "group", axis=0, tiled=True),
        lax.all_gather(query_weight, "group", axis=0, tiled=True),
        lax.all_gather(key_weight, "group", axis=0, tiled=True),
        lax.all_gather(value_weight, "group", axis=0, tiled=True),
        lax.all_gather(out_weight, "group", axis=0, tiled=True),
    )
    normed_attn_f, attn_norm_pull = jax.vjp(normalize, inputs, gain_attn.astype(jnp.float32))
    normed_attn = normed_attn_f.astype(jnp.bfloat16)
    query_pre = jnp.dot(normed_attn, weight_q, preferred_element_type=jnp.float32).reshape(
        tokens, HEADS, HEAD
    )
    key_pre = jnp.dot(normed_attn, weight_k, preferred_element_type=jnp.float32).reshape(
        tokens, KV_HEADS, HEAD
    )
    queries = rotate(query_pre, cosine, sine_table).astype(jnp.bfloat16)
    own_keys = rotate(key_pre, cosine, sine_table).astype(jnp.bfloat16)
    own_values = (
        jnp.dot(normed_attn, weight_v, preferred_element_type=jnp.float32)
        .astype(jnp.bfloat16)
        .reshape(tokens, KV_HEADS, HEAD)
    )
    prev_keys, prev_values = from_behind((own_keys, own_values), "group", 1)
    all_keys = jnp.concatenate([prev_keys, own_keys], 0)
    all_values = jnp.concatenate([prev_values, own_values], 0)
    query_blocks = queries.reshape(block_count, rows_block, KV_HEADS, groups, HEAD)
    position_blocks = positions.reshape(block_count, rows_block)

    def masked_scores(query_block, query_pos):
        scores = (
            jnp.einsum("qkgd,jkd->kgqj", query_block, all_keys, preferred_element_type=jnp.float32)
            * score_scale
        )
        visible = (key_positions[None, :] >= 0) & (
            (key_positions[None, :] <= query_pos[:, None]) | (key_positions[None, :] < prefix_len)
        )
        return jnp.where(visible, scores, MASKED)

    def forward_block(operands):
        query_block, query_pos = operands
        scores = masked_scores(query_block, query_pos)
        row_peak = jnp.max(scores, -1, keepdims=True)
        exponent = jnp.exp(scores - row_peak)
        row_total = jnp.sum(exponent, -1, keepdims=True)
        weights_low = (exponent / row_total).astype(jnp.bfloat16)
        attended_block = jnp.einsum(
            "kgqj,jkd->qkgd", weights_low, all_values, preferred_element_type=jnp.float32
        )
        return (attended_block.astype(jnp.bfloat16), row_peak + jnp.log(row_total))

    attended_blocks, log_totals = lax.map(forward_block, (query_blocks, position_blocks))
    attended = attended_blocks.reshape(tokens, HEADS * HEAD)
    residual = inputs + jnp.dot(attended, weight_o, preferred_element_type=jnp.float32)
    gain_ffn, router_full, expert_in_full, expert_out_full = (
        lax.all_gather(ffn_gain, "group", axis=0, tiled=True),
        lax.all_gather(router_weight, "group", axis=0, tiled=True),
        lax.all_gather(expert_in, "group", axis=0, tiled=True),
        lax.all_gather(expert_out, "group", axis=0, tiled=True),
    )
    normed_ffn_f, ffn_norm_pull = jax.vjp(normalize, residual, gain_ffn.astype(jnp.float32))
    normed_ffn = normed_ffn_f.astype(jnp.bfloat16)
    logits = jnp.dot(normed_ffn, router_full, preferred_element_type=jnp.float32)
    gate_probs = jax.nn.softmax(jnp.take_along_axis(logits, token_routes, 1), -1)
    expert_ids = jnp.arange(EXPERTS, dtype=jnp.int32)
    member = (token_routes[:, :, None] == expert_ids[None, None, :]).astype(jnp.int32)
    per_token = jnp.sum(member, 1)
    before = jnp.cumsum(per_token, 0) - per_token
    slot_index = jnp.sum(member * before[:, None, :], 2)
    flat_slot = (token_routes * CAP + slot_index).reshape(-1)
    token_ids = jnp.repeat(jnp.arange(tokens, dtype=jnp.int32), TOP)
    source = jnp.zeros((EXPERTS * CAP,), jnp.int32).at[flat_slot].set(token_ids)
    filled = jnp.zeros((EXPERTS * CAP,), jnp.bfloat16).at[flat_slot].set(1.0)
    gate_rows = jnp.zeros((EXPERTS * CAP,), jnp.float32).at[flat_slot].set(gate_probs.reshape(-1))
    buffer = (normed_ffn[source] * filled[:, None]).reshape(EXPERTS, CAP, width)
    gate_up, hidden, expert_rows = expert_forward(buffer, expert_in_full, expert_out_full)
    picked = expert_rows.reshape(EXPERTS * CAP, width)[flat_slot].reshape(tokens, TOP, width)
    block_out = (residual + jnp.sum(gate_probs[:, :, None] * picked, 1)).astype(jnp.bfloat16)
    grad_gates = jnp.sum(picked * grad_out[:, None, :], 2)
    grad_expert_rows = (
        (grad_out[source] * gate_rows[:, None]).astype(jnp.bfloat16).reshape(EXPERTS, CAP, width)
    )
    back_in, back_out = (
        lax.all_gather(expert_in, "group", axis=0, tiled=True),
        lax.all_gather(expert_out, "group", axis=0, tiled=True),
    )
    grad_buffer, grad_in_weight, grad_out_weight = expert_backward(
        buffer, gate_up, hidden, grad_expert_rows, back_in, back_out
    )
    expert_in_grad, expert_out_grad = (
        lax.psum_scatter(grad_in_weight, ("group", "replica"), scatter_dimension=1, tiled=True),
        lax.psum_scatter(grad_out_weight, ("group", "replica"), scatter_dimension=1, tiled=True),
    )
    grad_from_experts = jnp.sum(
        grad_buffer.reshape(EXPERTS * CAP, width)[flat_slot].reshape(tokens, TOP, width), 1
    )
    mean_term = jnp.sum(gate_probs * grad_gates, 1, keepdims=True)
    grad_chosen = gate_probs * (grad_gates - mean_term)
    grad_logits = jnp.sum(
        grad_chosen[:, :, None]
        * (token_routes[:, :, None] == expert_ids[None, None, :]).astype(jnp.float32),
        1,
    )
    router_f = router_full.astype(jnp.float32)
    router_full_grad = lax.dot_general(
        normed_ffn.astype(jnp.float32), grad_logits, (((0,), (0,)), ((), ())), precision=HIGHEST
    )
    grad_normed_ffn = grad_from_experts + lax.dot_general(
        grad_logits, router_f, (((1,), (1,)), ((), ())), precision=HIGHEST
    )
    grad_res_norm, ffn_gain_full_grad = ffn_norm_pull(grad_normed_ffn)
    grad_residual = grad_out + grad_res_norm
    grad_res_low = grad_residual.astype(jnp.bfloat16)
    out_full_grad = contract_rows(attended, grad_res_low)
    grad_attended = contract_cols(grad_res_low, weight_o).astype(jnp.bfloat16)
    grad_blocks = grad_attended.reshape(block_count, rows_block, KV_HEADS, groups, HEAD)

    def backward_block(running, operands):
        grad_key_sum, grad_value_sum = running
        query_block, query_pos, grad_block, log_total = operands
        scores = masked_scores(query_block, query_pos)
        probability = jnp.exp(scores - log_total)
        grad_probs = jnp.einsum(
            "qkgd,jkd->kgqj", grad_block, all_values, preferred_element_type=jnp.float32
        )
        row_delta = jnp.sum(probability * grad_probs, -1, keepdims=True)
        grad_scores = (probability * (grad_probs - row_delta)).astype(jnp.bfloat16)
        grad_query = (
            jnp.einsum("kgqj,jkd->qkgd", grad_scores, all_keys, preferred_element_type=jnp.float32)
            * score_scale
        )
        grad_key_sum = (
            grad_key_sum
            + jnp.einsum(
                "kgqj,qkgd->jkd", grad_scores, query_block, preferred_element_type=jnp.float32
            )
            * score_scale
        )
        grad_value_sum = grad_value_sum + jnp.einsum(
            "kgqj,qkgd->jkd",
            probability.astype(jnp.bfloat16),
            grad_block,
            preferred_element_type=jnp.float32,
        )
        return ((grad_key_sum, grad_value_sum), grad_query)

    empty_keys = jnp.zeros((2 * tokens, KV_HEADS, HEAD), jnp.float32)
    (grad_keys_all, grad_values_all), grad_query_blocks = lax.scan(
        backward_block,
        (empty_keys, empty_keys),
        (query_blocks, position_blocks, grad_blocks, log_totals),
    )
    back_keys, back_values = (
        from_behind(grad_keys_all[:tokens].astype(jnp.bfloat16), "group", -1).astype(jnp.float32),
        from_behind(grad_values_all[:tokens].astype(jnp.bfloat16), "group", -1).astype(jnp.float32),
    )
    grad_keys = grad_keys_all[tokens:] + back_keys
    grad_values = grad_values_all[tokens:] + back_values
    grad_query_pre = (
        rotate_back(grad_query_blocks.reshape(tokens, HEADS, HEAD), cosine, sine_table)
        .astype(jnp.bfloat16)
        .reshape(tokens, HEADS * HEAD)
    )
    grad_key_pre = (
        rotate_back(grad_keys, cosine, sine_table)
        .astype(jnp.bfloat16)
        .reshape(tokens, KV_HEADS * HEAD)
    )
    grad_value_pre = grad_values.astype(jnp.bfloat16).reshape(tokens, KV_HEADS * HEAD)
    query_full_grad = contract_rows(normed_attn, grad_query_pre)
    key_full_grad = contract_rows(normed_attn, grad_key_pre)
    value_full_grad = contract_rows(normed_attn, grad_value_pre)
    grad_normed_attn = (
        contract_cols(grad_query_pre, weight_q)
        + contract_cols(grad_key_pre, weight_k)
        + contract_cols(grad_value_pre, weight_v)
    )
    grad_in_norm, attn_gain_full_grad = attn_norm_pull(grad_normed_attn)
    input_grad = grad_residual + grad_in_norm
    attn_gain_grad, query_grad, key_grad, value_grad, out_grad, ffn_gain_grad, router_grad = (
        lax.psum_scatter(
            attn_gain_full_grad, ("group", "replica"), scatter_dimension=0, tiled=True
        ),
        lax.psum_scatter(query_full_grad, ("group", "replica"), scatter_dimension=0, tiled=True),
        lax.psum_scatter(key_full_grad, ("group", "replica"), scatter_dimension=0, tiled=True),
        lax.psum_scatter(value_full_grad, ("group", "replica"), scatter_dimension=0, tiled=True),
        lax.psum_scatter(out_full_grad, ("group", "replica"), scatter_dimension=1, tiled=True),
        lax.psum_scatter(ffn_gain_full_grad, ("group", "replica"), scatter_dimension=0, tiled=True),
        lax.psum_scatter(router_full_grad, ("group", "replica"), scatter_dimension=0, tiled=True),
    )
    return (
        block_out[None],
        input_grad[None],
        attn_gain_grad,
        query_grad,
        key_grad,
        value_grad,
        out_grad,
        ffn_gain_grad,
        router_grad,
        expert_in_grad,
        expert_out_grad,
    )


def solution(mesh):
    placed = (
        P("replica", "group", None),
        P("group"),
        P("group", None),
        P("group", None),
        P("group", None),
        P("group", None),
        P("group"),
        P("group", None),
        P("group", None, None),
        P("group", None, None),
        P("replica", "group", None),
        P("replica"),
        P("replica", "group", None),
    )
    return jax.shard_map(
        on_device,
        mesh=mesh,
        in_specs=placed,
        out_specs=(
            P("replica", "group", None),
            P("replica", "group", None),
            P(("group", "replica")),
            P(("group", "replica"), None),
            P(("group", "replica"), None),
            P(("group", "replica"), None),
            P(None, ("group", "replica")),
            P(("group", "replica")),
            P(("group", "replica"), None),
            P(None, ("group", "replica"), None),
            P(None, ("group", "replica"), None),
        ),
        check_vma=False,
    )
```

profile of v0, /device:TPU:1, one launch (start us, length us, event | category | flops | bytes accessed | tf_op | source)
XLA Modules:
  0.0 2654.7 jit_solution(8985328769214327289)
XLA Ops:
  12.5 3.7 all-gather
  16.2 3.2 all-gather.1
  20.0 3.9 all_gather.35
  26.8 28.6 %scatter_custom_fusion.1 = bf16[6144]{0:T(1024)(128)(2,1)S(1)} fusion(s32[4096]{0:T(1024)S(1)} %bitcast.237, bf16[4096]{0:T(1024)(128)(2,1)S(1)} %broadcast.399, bf16[]{:T(256)} %constant.114.clone.1), kind=kCustom, calls=%fused_computation.149 | custom fusion | bytes 12290 | tf_op jit(solution)/shard_map/scatter | solution.py:204
  57.8 15.5 scatter_custom_fusion
  73.4 1.5 bitcast_convert_fusion
  74.9 27.4 %gather_fusion.2 = f32[6144,1024]{1,0:T(8,128)} fusion(f32[512,1024]{1,0:T(8,128)S(1)} %bitcast_convert_fusion, s32[6144]{0:T(1024)S(1)} %fusion.64), kind=kCustom, calls=%fused_computation.2 | custom fusion | bytes 50356224 | tf_op jit(solution)/shard_map/gather | solution.py:212
  102.2 24.8 copy.88
  127.3 1.6 or_and_fusion
  129.0 2.9 convolution_convert_fusion.1
  131.9 4.3 collective-permute-start
  136.1 1.8 copy.75
  139.9 2.3 collective-permute-start.1
  142.3 4.3 copy.76
  146.6 3.7 fusion.45
  150.8 3.2 collective-permute-done.1
  154.0 17.8 fusion.91
  171.8 14.2 fusion.3
  186.0 13.8 fusion.41
  199.9 3.3 multiply_reduce_fusion.2
  204.8 26.8 %gather_fusion = bf16[6144,1024]{1,0:T(8,128)(2,1)} fusion(bf16[512,1024]{1,0:T(8,128)(2,1)S(1)} %multiply_convert_fusion.6, s32[6144]{0:T(1024)S(1)} %fusion.64), kind=kCustom, calls=%fused_computation | custom fusion | bytes 25190400 | tf_op jit(solution)/shard_map/gather | solution.py:206
  232.4 33.0 %gather_fusion.4 = f32[4096]{0:T(1024)S(1)} fusion(f32[512,16]{0,1:T(8,128)S(1)} %fusion.92, s32[4096]{0:T(1024)S(1)} %copy-done.4), kind=kCustom, calls=%fused_computation.4 | custom fusion | bytes 65536 | tf_op jit(solution)/shard_map/jit(take_along_axis)/gather | solution.py:195
  266.6 16.1 scatter_custom_fusion.2
  282.7 15.5 copy.85
  299.8 218.3 %all-gather.17.cloned.1.call-done = bf16[16,1024,1024]{2,1,0:T(8,128)(2,1)} async-done(((bf16[8,1024,1024]{2,1,0:T(8,128)(2,1)}), bf16[16,1024,1024]{2,1,0:T(8,128)(2,1)}) %all-gather.17.cloned.1.call-update) | async-done | bytes 33554448 | tf_op jit(solution)/shard_map/all_gather | solution.py:189
  518.1 30.7 %fusion.14 = f32[16,384,1024]{2,1,0:T(8,128)} fusion(bf16[16,1024,1024]{2,1,0:T(8,128)(2,1)} %all-gather.17.cloned.1.call-done, bf16[16,384,1024]{1,2,0:T(8,128)(2,1)} %copy.85, bf16[16,384]{1,0:T(8,128)(2,1)S(1)} %copy-done.38), kind=kOutput, calls=%fused_computation.36 | convolution fusion | flops 12891193344 | bytes 71315456 | tf_op jit(solution)/shard_map/ecd,edf->ecf/dot_general | solution.py:76
  548.8 171.8 %all-gather.19.cloned.1.call-done = bf16[16,1024,512]{2,1,0:T(8,128)(2,1)} async-done(((bf16[8,1024,512]{2,1,0:T(8,128)(2,1)}), bf16[16,1024,512]{2,1,0:T(8,128)(2,1)}) %all-gather.19.cloned.1.call-update) | async-done | bytes 16777232 | tf_op jit(solution)/shard_map/all_gather | solution.py:190
  720.6 30.4 %multiply_convert_fusion.2 = (bf16[16,384,512]{2,1,0:T(8,128)(2,1)}, bf16[16,384,512]{2,1,0:T(8,128)(2,1)}, bf16[16,384,512]{2,1,0:T(8,128)(2,1)}) fusion(f32[16,384,1024]{2,1,0:T(8,128)} %fusion.14, bf16[16,1024,512]{2,1,0:T(8,128)(2,1)} %all-gather.19.cloned.1.call-done, f32[16,384,1024]{1,2,0:T(8,128)} %copy.88, f32[16,384]{1,0:T(8,128)S(1)} %mul.437), kind=kOutput, calls=%fused_computation.30 | convolution fusion | flops 6502219776 | bytes 86007808 | tf_op jit(solution)/shard_map/ecd,edf->ecf/dot_general | solution.py:83
  750.9 26.2 fusion.16
  777.2 30.5 %gather_fusion.3 = f32[4096,1024]{1,0:T(8,128)} fusion(f32[6144,1024]{1,0:T(8,128)} %bitcast.198, s32[4096]{0:T(1024)S(1)} %copy-done.44), kind=kCustom, calls=%fused_computation.3 | custom fusion | bytes 33570816 | tf_op jit(solution)/shard_map/gather | solution.py:226
  807.6 9.7 bitcast_reduce_fusion
  817.3 22.7 fusion.93
  840.0 30.6 %gather_fusion.1 = f32[4096,1024]{1,0:T(8,128)} fusion(f32[6144,1024]{1,0:T(8,128)} %bitcast.197, s32[4096]{0:T(1024)S(1)} %copy-done.44), kind=kCustom, calls=%fused_computation.1 | custom fusion | bytes 33570816 | tf_op jit(solution)/shard_map/gather | solution.py:208
  870.6 10.8 fusion.8
  883.6 2.0 fusion.96
  885.6 3.9 multiply_reduce_fusion
  889.6 1.6 fusion.34
  891.2 1.3 copy-done.10
  894.6 13.3 fusion.38
  908.0 1.3 collective-permute-start.3
  909.3 22.9 fusion
  933.6 2.3 fusion.51
  936.0 27.5 %fusion.2 = bf16[8,2,512,1024]{2,3,1,0:T(8,128)(2,1)} fusion(f32[8,1024,512,2]{2,1,3,0:T(8,128)} %get-tuple-element.105, f32[8,2,512,1024]{2,3,1,0:T(8,128)} %get-tuple-element.100, f32[8,2,512]{2,1,0:T(2,128)S(1)} %get-tuple-element.104, f32[8,2,512]{2,1,0:T(2,128)S(1)} %bitcast.222), kind=kLoop, calls=%fused_computation.12 | loop fusion | flops 33554432 | bytes 83951616 | tf_op jit(solution)/shard_map/while/body/eval_jaxpr/convert_element_type | solution.py:258
  963.5 11.3 fusion.37
  974.9 1.3 collective-permute-start.2
  976.2 13.4 collective-permute-done.2
  990.8 2.2 fusion.53
  993.1 4.5 fusion.58
  998.5 9.0 convolution_multiply_fusion
  1008.9 3.4 fusion.49
  1013.1 24.6 fusion.19
  1038.4 33.7 %fusion.12 = f32[16,1024,1024]{2,1,0:T(8,128)} fusion(bf16[16,384,1024]{1,2,0:T(8,128)(2,1)} %copy.85, bf16[16,384,512]{2,1,0:T(8,128)(2,1)} %get-tuple-element.71, bf16[16,384,512]{2,1,0:T(8,128)(2,1)} %get-tuple-element.70, bf16[16,384]{1,0:T(8,128)(2,1)S(1)} %copy-done.39), kind=kOutput, calls=%fused_computation.34 | convolution fusion | flops 12916359168 | bytes 92286976 | tf_op jit(solution)/shard_map/ecd,ecf->edf/dot_general | solution.py:95
  1072.1 4.5 fusion.94
  1076.6 1.4 copy.107
  1078.0 2.3 fusion.95
  1080.5 2.5 fusion.29
  1083.1 40.6 %all-reduce.2 = (f32[1024]{0:T(1024)S(1)}, f32[1024]{0:T(1024)S(1)}) all-reduce(f32[1024]{0:T(1024)S(1)} %get-tuple-element.66, f32[1024]{0:T(1024)S(1)} %copy-done.60), channel_id=2, replica_groups=mesh['group'=2,'replica'=16] {'group','replica'}, use_global_device_ids=true, to_apply=%region_22.23.clone | all-reduce | flops 2048 | bytes 16384
  1124.9 3.5 fusion.36
  1128.3 31.6 %reduce-scatter.14.cloned.1.call-done = f32[32,512]{1,0:T(8,128)} async-done(((f32[1024,512]{1,0:T(8,128)}), f32[32,512]{1,0:T(8,128)}) %reduce-scatter.14.cloned.1.call-update) | async-done | bytes 65552 | tf_op jit(solution)/shard_map/reduce_scatter | solution.py:317
  1159.9 136.1 %reduce-scatter.12.cloned.1.call-done = f32[32,512]{1,0:T(8,128)} async-done(((f32[1024,512]{1,0:T(8,128)}), f32[32,512]{1,0:T(8,128)}) %reduce-scatter.12.cloned.1.call-update) | async-done | bytes 65552 | tf_op jit(solution)/shard_map/reduce_scatter | solution.py:316
  1296.0 139.9 %reduce-scatter.16.cloned.1.call-done = f32[1024,32]{0,1:T(8,128)} async-done(((f32[1024,1024]{0,1:T(8,128)}), f32[1024,32]{0,1:T(8,128)}) %reduce-scatter.16.cloned.1.call-update) | async-done | bytes 131088 | tf_op jit(solution)/shard_map/reduce_scatter | solution.py:318
  1435.9 140.7 %reduce-scatter.10.cloned.1.call-done = f32[32,1024]{1,0:T(8,128)} async-done(((f32[1024,1024]{1,0:T(8,128)}), f32[32,1024]{1,0:T(8,128)}) %reduce-scatter.10.cloned.1.call-update) | async-done | bytes 131088 | tf_op jit(solution)/shard_map/reduce_scatter | solution.py:315
  1576.6 362.2 %reduce-scatter.20.cloned.1.call-done = f32[16,32,512]{2,1,0:T(8,128)} async-done(((f32[16,1024,512]{2,1,0:T(8,128)}), f32[16,32,512]{2,1,0:T(8,128)}) %reduce-scatter.20.cloned.1.call-update) | async-done | bytes 1048592 | tf_op jit(solution)/shard_map/reduce_scatter | solution.py:223
  1938.8 709.0 %reduce-scatter.18.cloned.1.call-done = f32[16,32,1024]{2,1,0:T(8,128)} async-done(((f32[16,1024,1024]{2,1,0:T(8,128)}), f32[16,32,1024]{2,1,0:T(8,128)}) %reduce-scatter.18.cloned.1.call-update) | async-done | bytes 2097168 | tf_op jit(solution)/shard_map/reduce_scatter | solution.py:222
  (231 shorter events, 30.1 us)
Async XLA Ops:
  7.2 121.8 %all-gather.9.cloned.1.call-start = ((), (), s32[]{:S(2)}) async-start(), calls=%async_computation.7 | async-start | bytes 1572864 | tf_op jit(solution)/shard_map/all_gather | solution.py:137
  7.9 128.2 %all-gather.11.cloned.1.call-start = ((), (), s32[]{:S(2)}) async-start(), calls=%async_computation.8 | async-start | bytes 1572864 | tf_op jit(solution)/shard_map/all_gather | solution.py:136
  8.7 133.6 %all-gather.13.cloned.1.call-start = ((), (), s32[]{:S(2)}) async-start(), calls=%async_computation.9 | async-start | bytes 3145728 | tf_op jit(solution)/shard_map/all_gather | solution.py:135
  9.4 190.5 %all-gather.15.cloned.1.call-start = ((), (), s32[]{:S(2)}) async-start(), calls=%async_computation.10 | async-start | bytes 3145728 | tf_op jit(solution)/shard_map/all_gather | solution.py:138
  10.0 508.1 %all-gather.17.cloned.1.call-start = ((), (), s32[]{:S(2)}) async-start(), calls=%async_computation.11 | async-start | bytes 50331648 | tf_op jit(solution)/shard_map/all_gather | solution.py:189
  10.6 1.8 copy-start.61
  10.6 5.6 copy-start.62
  10.6 9.4 copy-start.59
  10.6 710.0 %all-gather.19.cloned.1.call-start = ((), (), s32[]{:S(2)}) async-start(), calls=%async_computation.12 | async-start | bytes 25165824 | tf_op jit(solution)/shard_map/all_gather | solution.py:190
  11.2 1065.4 %reduce-scatter.22.cloned.1.call-start = ((), (), s32[]{:S(2)}) async-start(), calls=%async_computation.19 | async-start | bytes 540672
  11.5 61.9 %copy-start.14 = (s32[1,512,8]{2,1,0:T(8,128)}, s32[1,512,8]{2,1,0:T(8,128)S(1)}, u32[]{:S(2)}) copy-start(s32[1,512,8]{2,1,0:T(8,128)S(1)} %copy.78) | copy-start | bytes 49156
  12.4 13.0 copy-start.55
  12.4 134.2 %copy-start.51 = (f32[512]{0:T(512)}, f32[512]{0:T(512)S(1)}, u32[]{:S(2)}) copy-start(f32[512]{0:T(512)S(1)} %fusion.74) | copy-start | bytes 6148
  16.2 130.4 %copy-start.45 = (f32[2,1,512]{2,1,0:T(1,128)}, f32[2,1,512]{2,1,0:T(1,128)S(1)}, u32[]{:S(2)}) copy-start(f32[2,1,512]{2,1,0:T(1,128)S(1)} %convert_element_type.171) | copy-start | bytes 12292
  26.2 47.2 %copy-start.48 = (s32[4096,1]{0,1:T(1,128)}, s32[4096,1]{0,1:T(1,128)S(1)}, u32[]{:S(2)}) copy-start(s32[4096,1]{0,1:T(1,128)S(1)} %compare_select_fusion.1) | copy-start | bytes 49156
  74.9 27.4 %copy-start = (f32[512,1024]{1,0:T(8,128)}, f32[512,1024]{1,0:T(8,128)S(1)}, u32[]{:S(2)}) copy-start(f32[512,1024]{1,0:T(8,128)S(1)} %bitcast_convert_fusion) | copy-start | bytes 6291460
  127.3 23.1 copy-start.28
  127.3 23.1 copy-start.30
  131.9 54.1 %collective-permute-start = (bf16[512,8,64]{0,2,1:T(8,128)(2,1)}, bf16[512,8,64]{0,2,1:T(8,128)(2,1)}, u32[]{:S(2)}, u32[]{:S(2)}) collective-permute-start(bf16[512,8,64]{0,2,1:T(8,128)(2,1)} %bitcast.2), channel_id=1, source_target_pairs={{0,16},{1,17},{2,18},{3,19},{4,20},{5,21},{6,22},{7,23},{8,24},{9,... | collective-permute-start | bytes 1572872 | tf_op jit(solution)/shard_map/ppermute | solution.py:23
  139.0 15.0 copy-start.21
  139.0 15.0 copy-start.23
  139.9 14.1 collective-permute-start.1
  150.4 3.6 copy-start.37
  150.8 21.0 copy-start.25
  150.8 21.0 copy-start.26
  199.8 3.4 copy-start.13
  199.9 4.7 copy-start.49
  203.2 1.6 copy-start.57
  203.2 1.5 copy-start.53
  204.8 26.8 %copy-start.2 = (bf16[512,1024]{1,0:T(8,128)(2,1)}, bf16[512,1024]{1,0:T(8,128)(2,1)S(1)}, u32[]{:S(2)}) copy-start(bf16[512,1024]{1,0:T(8,128)(2,1)S(1)} %multiply_convert_fusion.6) | copy-start | bytes 3145732
  204.8 26.8 %copy-start.40 = (bf16[1024,16]{0,1:T(8,128)(2,1)S(1)}, bf16[1024,16]{0,1:T(8,128)(2,1)}, u32[]{:S(2)}) copy-start(bf16[1024,16]{0,1:T(8,128)(2,1)} %all_gather.35) | copy-start | bytes 98308
  232.4 33.2 %copy-start.15 = (s32[1,512,8]{2,1,0:T(8,128)S(1)}, s32[1,512,8]{2,1,0:T(8,128)}, u32[]{:S(2)}) copy-start(s32[1,512,8]{2,1,0:T(8,128)} %copy-done.14) | copy-start | bytes 49156
  282.7 437.9 %copy-start.42 = (f32[16,384]{1,0:T(8,128)}, f32[16,384]{1,0:T(8,128)S(1)}, u32[]{:S(2)}) copy-start(f32[16,384]{1,0:T(8,128)S(1)} %mul.437) | copy-start | bytes 73732
  282.7 235.4 %copy-start.38 = (bf16[16,384]{1,0:T(8,128)(2,1)S(1)}, bf16[16,384]{1,0:T(8,128)(2,1)}, u32[]{:S(2)}) copy-start(bf16[16,384]{1,0:T(8,128)(2,1)} %mul.431) | copy-start | bytes 36868
  750.9 26.2 copy-start.44
  807.6 9.7 copy-start.7
  840.0 30.6 %copy-start.1 = (f32[512,1024]{1,0:T(8,128)S(1)}, f32[512,1024]{1,0:T(8,128)}, u32[]{:S(2)}) copy-start(f32[512,1024]{1,0:T(8,128)} %copy-done) | copy-start | bytes 6291460
  840.0 30.6 %copy-start.19 = (f32[512,8]{1,0:T(8,128)S(1)}, f32[512,8]{1,0:T(8,128)}, u32[]{:S(2)}) copy-start(f32[512,8]{1,0:T(8,128)} %fusion.61) | copy-start | bytes 49156
  870.6 12.9 copy-start.36
  881.4 2.2 copy-start.3
  881.4 4.2 copy-start.9
  881.4 4.2 copy-start.41
  881.4 4.2 copy-start.50
  881.4 4.2 copy-start.54
  885.6 3.9 copy-start.58
  885.6 4.0 copy-start.12
  885.6 4.0 copy-start.20
  889.6 3.0 copy-start.27
  894.4 265.4 %reduce-scatter.14.cloned.1.call-start = ((), (), s32[]{:S(2)}) async-start(), calls=%async_computation.15 | async-start | bytes 2162688 | tf_op jit(solution)/shard_map/reduce_scatter | solution.py:317
  908.0 24.3 collective-permute-start.3
  935.9 360.1 %reduce-scatter.12.cloned.1.call-start = ((), (), s32[]{:S(2)}) async-start(), calls=%async_computation.14 | async-start | bytes 2162688 | tf_op jit(solution)/shard_map/reduce_scatter | solution.py:316
  974.8 15.0 copy-start.29
  974.8 15.0 copy-start.31
  974.9 14.7 collective-permute-start.2
  990.8 2.3 copy-start.11
  993.1 442.8 %reduce-scatter.16.cloned.1.call-start = ((), (), s32[]{:S(2)}) async-start(), calls=%async_computation.16 | async-start | bytes 4325376 | tf_op jit(solution)/shard_map/reduce_scatter | solution.py:318
  997.6 579.0 %reduce-scatter.10.cloned.1.call-start = ((), (), s32[]{:S(2)}) async-start(), calls=%async_computation.13 | async-start | bytes 4325376 | tf_op jit(solution)/shard_map/reduce_scatter | solution.py:315
  1012.4 926.4 %reduce-scatter.20.cloned.1.call-start = ((), (), s32[]{:S(2)}) async-start(), calls=%async_computation.18 | async-start | bytes 34603008 | tf_op jit(solution)/shard_map/reduce_scatter | solution.py:223
  1037.7 1610.0 %reduce-scatter.18.cloned.1.call-start = ((), (), s32[]{:S(2)}) async-start(), calls=%async_computation.17 | async-start | bytes 69206016 | tf_op jit(solution)/shard_map/reduce_scatter | solution.py:222
  1078.0 2.3 copy-start.18
  1078.0 2.3 copy-start.24
  1078.0 2.5 copy-start.32
  1080.5 2.6 copy-start.60
  1080.5 44.3 %copy-start.56 = (f32[512]{0:T(512)S(1)}, f32[512]{0:T(512)}, u32[]{:S(2)}) copy-start(f32[512]{0:T(512)} %copy-done.55) | copy-start | bytes 6148
  (16 other events, 16.8 us)
Sparse Core Ops, SparseCore 0:
  9.6 23.7 all-gather.8
  34.9 21.3 all-gather.10
  57.8 33.1 all-gather.12
  92.3 33.1 all-gather.14
  126.9 391.1 all-gather.16
  519.5 201.0 all-gather.18
  894.6 129.0 reduce-scatter.21
  1026.6 133.2 reduce-scatter.13
  1162.7 133.2 reduce-scatter.11
  1298.8 137.0 reduce-scatter.15
  1438.8 137.7 reduce-scatter.9
  1579.4 359.2 reduce-scatter.19
  1941.8 705.8 reduce-scatter.17
where the time goes:
time: 2660 us; the launch traced here: 2650 us
  waiting for transfers between devices  1930 us (73%)
  matrix products  296 us (11%)
  local copies, waits for them, and re-layouts  271 us (10%)
  other arithmetic  79.3 us (3%)
  blocking collectives  51.4 us (2%)
    reduce_scatter x1, waiting for transfers between devices, on_device(): lax.psum_scatter(grad_in_weight, ('group', 'replica'), scatter_dimension=...  709 us
    reduce_scatter x1, waiting for transfers between devices, on_device(): lax.psum_scatter(grad_out_weight, ('group', 'replica'), scatter_dimension...  362 us
    all_gather x1, waiting for transfers between devices, on_device(): lax.all_gather(expert_in, 'group', axis=0, tiled=True)  218 us
    all_gather x1, waiting for transfers between devices, on_device(): lax.all_gather(expert_out, 'group', axis=0, tiled=True)  172 us
    reduce_scatter x1, waiting for transfers between devices, on_device(): lax.psum_scatter(query_full_grad, ('group', 'replica'), scatter_dimension...  141 us
    reduce_scatter x1, waiting for transfers between devices, on_device(): lax.psum_scatter(out_full_grad, ('group', 'replica'), scatter_dimension=1...  140 us
    reduce_scatter x1, waiting for transfers between devices, on_device(): lax.psum_scatter(key_full_grad, ('group', 'replica'), scatter_dimension=0...  136 us
  transfers between devices with their start and end apart: 17, of which 10 were waited for; matrix products, arithmetic and copies ran while one was open for 18% of the time, Pallas kernels for 0%

commit v1 on v0

--- a/solution.py
+++ b/solution.py
@@ -3,6 +3,7 @@
 import jax.numpy as jnp
 from jax import lax
 from jax.sharding import PartitionSpec as P
+from jax.lax import axis_index, ppermute, psum
 
 HEADS = 16
 KV_HEADS = 8
@@ -15,6 +16,30 @@
 THETA_BASE = 10000.0
 MASKED = -1e30
 HIGHEST = lax.Precision.HIGHEST
+
+
+def rest_squares(local, d0):
+    local = jnp.moveaxis(local, 0, d0)
+    raw_out = local.shape
+    return local.reshape(*raw_out[:d0], raw_out[d0] * raw_out[d0 + 1], *raw_out[d0 + 2 :])
+
+
+def solve_slot(load, across):
+    lower = psum(1, axis_name=across)
+    known = axis_index(across)
+    moved, front = (lower, known)
+    s_next, carry = (load[None], 1)
+    while carry < moved:
+        pages = []
+        for to_i in range(moved):
+            pages.append((to_i, to_i ^ carry))
+        y_new = ppermute(s_next, axis_name=across, perm=pages)
+        item_now = front & carry == 0
+        opened = jnp.where(item_now, s_next, y_new)
+        w2 = jnp.where(item_now, y_new, s_next)
+        s_next = jnp.concatenate([opened, w2])
+        carry *= 2
+    return s_next
 
 
 def from_behind(value, axis, steps):
@@ -116,6 +141,11 @@
     prefix,
     cotangent,
 ):
+
+    def scan_leaves_for(local_x, a0, d_out):
+        carry_in = solve_slot(local_x, a0)
+        return rest_squares(carry_in, d_out)
+
     tokens = block_in.shape[1]
     width = block_in.shape[2]
     half_index = lax.axis_index("group")
@@ -186,7 +216,7 @@
     gain_ffn, router_full, expert_in_full, expert_out_full = (
         lax.all_gather(ffn_gain, "group", axis=0, tiled=True),
         lax.all_gather(router_weight, "group", axis=0, tiled=True),
-        lax.all_gather(expert_in, "group", axis=0, tiled=True),
+        scan_leaves_for(expert_in, "group", 0),
         lax.all_gather(expert_out, "group", axis=0, tiled=True),
     )
     normed_ffn_f, ffn_norm_pull = jax.vjp(normalize, residual, gain_ffn.astype(jnp.float32))

time: 2660 us -> 3010 us (1.13)
  blocking collectives: 51.4 us -> 675 us
  waiting for transfers between devices: 1930 us -> 1620 us
  other arithmetic: 79.3 us -> 124 us
    all_gather x1, blocking collectives: 3.74 us -> 624 us  [on_device(): lax.all_gather(attn_gain, 'group', axis=0, tiled=True)]
    all_gather x1, waiting for transfers between devices: 218 us -> 0.02 us  [on_device(): lax.all_gather(expert_in, 'group', axis=0, tiled=True)]
    all_gather x1, waiting for transfers between devices: 172 us -> 0.01 us  [on_device(): lax.all_gather(expert_out, 'group', axis=0, tiled=True)]
    reduce_scatter x1, waiting for transfers between devices: 31.6 us -> 136 us  [on_device(): lax.psum_scatter(value_full_grad, ('group', 'replica'), scatter_dimension...]
    reduce_scatter x1, waiting for transfers between devices: 136 us -> 80.4 us  [on_device(): lax.psum_scatter(key_full_grad, ('group', 'replica'), scatter_dimension=0...]
  transfers between devices with their start and end apart: 17 -> 18, of which waited for: 10 -> 10; matrix products, arithmetic and copies ran while one was open for 18% -> 18% of each run, Pallas kernels for 0% -> 0%
where the time goes in v1:
time: 3010 us; the launch traced here: 3000 us
  waiting for transfers between devices  1620 us (54%)
  blocking collectives  675 us (22%)
  matrix products  282 us (9%)
  local copies, waits for them, and re-layouts  273 us (9%)
  other arithmetic  124 us (4%)
    reduce_scatter x1, waiting for transfers between devices, on_device(): lax.psum_scatter(grad_in_weight, ('group', 'replica'), scatter_dimension=...  709 us
    all_gather x1, blocking collectives, on_device(): lax.all_gather(attn_gain, 'group', axis=0, tiled=True)  624 us
    reduce_scatter x1, waiting for transfers between devices, on_device(): lax.psum_scatter(grad_out_weight, ('group', 'replica'), scatter_dimension...  363 us
    reduce_scatter x1, waiting for transfers between devices, on_device(): lax.psum_scatter(query_full_grad, ('group', 'replica'), scatter_dimension...  140 us
    reduce_scatter x1, waiting for transfers between devices, on_device(): lax.psum_scatter(out_full_grad, ('group', 'replica'), scatter_dimension=1...  140 us
    reduce_scatter x1, waiting for transfers between devices, on_device(): lax.psum_scatter(value_full_grad, ('group', 'replica'), scatter_dimension...  136 us
    reduce_scatter x1, waiting for transfers between devices, on_device(): lax.psum_scatter(key_full_grad, ('group', 'replica'), scatter_dimension=0...  80.4 us
  transfers between devices with their start and end apart: 18, of which 10 were waited for; matrix products, arithmetic and copies ran while one was open for 18% of the time, Pallas kernels for 0%

profile of v1, /device:TPU:1, one launch (start us, length us, event | category | flops | bytes accessed | tf_op | source)
XLA Modules:
  0.0 2996.9 jit_solution(10986001346835998087)
XLA Ops:
  11.2 2.1 collective-permute-start.2
  13.3 624.3 %all-gather = bf16[2,1,512]{2,1,0:T(2,128)(2,1)S(1)} all-gather(bf16[1,1,512]{2,1,0:T(2,128)(2,1)S(1)} %reshape.599), channel_id=1, replica_groups=mesh['group'=2,'replica'=16] {'group'}, dimensions={0}, use_global_device_ids=true | all-gather | bytes 3072 | tf_op jit(solution)/shard_map/all_gather | solution.py:164
  638.4 4.3 all-gather.1
  647.5 15.5 scatter_custom_fusion
  663.0 28.6 scatter_custom_fusion.1
  692.5 27.2 gather_fusion.2
  719.8 24.8 copy.88
  744.6 4.0 all_gather.34
  749.9 1.6 or_and_fusion
  751.5 1.5 copy.75
  755.0 4.2 collective-permute-start.1
  759.2 2.1 convolution_convert_fusion.1
  761.3 1.5 collective-permute-start
  762.9 3.9 copy.76
  766.8 3.0 fusion.45
  770.2 9.5 collective-permute-done.1
  779.7 14.5 fusion.91
  794.2 13.1 fusion.3
  807.4 13.9 fusion.41
  821.4 3.3 multiply_reduce_fusion.2
  826.3 26.9 gather_fusion
  853.6 33.0 %gather_fusion.4 = f32[4096]{0:T(1024)S(1)} fusion(f32[512,16]{0,1:T(8,128)S(1)} %fusion.92, s32[4096]{0:T(1024)S(1)} %copy-done.4), kind=kCustom, calls=%fused_computation.4 | custom fusion | bytes 65536 | tf_op jit(solution)/shard_map/jit(take_along_axis)/gather | solution.py:225
  887.8 15.7 scatter_custom_fusion.2
  903.5 17.1 copy.85
  922.2 22.6 broadcast_select_fusion.1
  944.8 22.7 pad_maximum_fusion
  967.5 28.1 fusion.14
  995.7 30.3 %multiply_convert_fusion.2 = (bf16[16,384,512]{2,1,0:T(8,128)(2,1)}, bf16[16,384,512]{2,1,0:T(8,128)(2,1)}, bf16[16,384,512]{2,1,0:T(8,128)(2,1)}) fusion(f32[16,384,1024]{2,1,0:T(8,128)} %fusion.14, bf16[16,1024,512]{2,1,0:T(8,128)(2,1)} %all-gather.17.cloned.1.call-done, f32[16,384,1024]{1,2,0:T(8,128)} %copy.88, f32[16,384]{1,0:T(8,128)S(1)} %mul.437), kind=kOutput, calls=%fused_computation.33 | convolution fusion | flops 6502219776 | bytes 86007808 | tf_op jit(solution)/shard_map/ecd,edf->ecf/dot_general | solution.py:108
  1026.0 18.3 fusion.93
  1044.3 30.6 %gather_fusion.1 = f32[4096,1024]{1,0:T(8,128)} fusion(f32[6144,1024]{1,0:T(8,128)} %bitcast.198, s32[4096]{0:T(1024)S(1)} %copy-done.51), kind=kCustom, calls=%fused_computation.1 | custom fusion | bytes 33570816 | tf_op jit(solution)/shard_map/gather | solution.py:238
  1075.0 10.8 fusion.8
  1086.2 26.4 fusion.16
  1112.6 30.5 %gather_fusion.3 = f32[4096,1024]{1,0:T(8,128)} fusion(f32[6144,1024]{1,0:T(8,128)} %bitcast.199, s32[4096]{0:T(1024)S(1)} %copy-done.51), kind=kCustom, calls=%fused_computation.3 | custom fusion | bytes 33570816 | tf_op jit(solution)/shard_map/gather | solution.py:256
  1143.1 8.2 bitcast_reduce_fusion
  1151.4 2.2 multiply_reduce_fusion
  1153.6 1.6 fusion.34
  1158.4 21.7 fusion
  1180.1 27.8 fusion.2
  1208.0 12.3 fusion.37
  1220.3 2.2 slice.125
  1223.8 2.0 fusion.96
  1225.9 7.0 collective-permute-done.3
  1232.9 1.5 slice_add_fusion.1
  1235.5 2.3 fusion.53
  1237.8 14.7 fusion.38
  1253.8 1.4 collective-permute-start.4
  1255.2 9.0 collective-permute-done.4
  1265.7 2.3 fusion.51
  1268.3 8.9 convolution_multiply_fusion
  1278.6 3.4 fusion.49
  1283.3 4.9 fusion.58
  1288.9 24.6 fusion.19
  1314.2 33.6 %fusion.12 = f32[16,1024,1024]{2,1,0:T(8,128)} fusion(bf16[16,384,1024]{1,2,0:T(8,128)(2,1)} %copy.85, bf16[16,384,512]{2,1,0:T(8,128)(2,1)} %get-tuple-element.71, bf16[16,384,512]{2,1,0:T(8,128)(2,1)} %get-tuple-element.70, bf16[16,384]{1,0:T(8,128)(2,1)S(1)} %copy-done.46), kind=kOutput, calls=%fused_computation.37 | convolution fusion | flops 12916359168 | bytes 92286976 | tf_op jit(solution)/shard_map/ecd,ecf->edf/dot_general | solution.py:120
  1347.9 18.0 reduce-scatter.22.cloned.1.call-done
  1367.3 3.0 fusion.94
  1371.5 2.5 fusion.29
  1374.0 42.5 %all-reduce.2 = (f32[1024]{0:T(1024)S(1)}, f32[1024]{0:T(1024)S(1)}) all-reduce(f32[1024]{0:T(1024)S(1)} %get-tuple-element.66, f32[1024]{0:T(1024)S(1)} %copy-done.67), channel_id=2, replica_groups=mesh['group'=2,'replica'=16] {'group','replica'}, use_global_device_ids=true, to_apply=%region_22.23.clone | all-reduce | flops 2048 | bytes 16384
  1417.7 4.1 fusion.36
  1421.8 80.4 %reduce-scatter.12.cloned.1.call-done = f32[32,512]{1,0:T(8,128)} async-done(((f32[1024,512]{1,0:T(8,128)}), f32[32,512]{1,0:T(8,128)}) %reduce-scatter.12.cloned.1.call-update) | async-done | bytes 65552 | tf_op jit(solution)/shard_map/reduce_scatter | solution.py:346
  1502.1 135.8 %reduce-scatter.14.cloned.1.call-done = f32[32,512]{1,0:T(8,128)} async-done(((f32[1024,512]{1,0:T(8,128)}), f32[32,512]{1,0:T(8,128)}) %reduce-scatter.14.cloned.1.call-update) | async-done | bytes 65552 | tf_op jit(solution)/shard_map/reduce_scatter | solution.py:347
  1638.0 140.3 %reduce-scatter.10.cloned.1.call-done = f32[32,1024]{1,0:T(8,128)} async-done(((f32[1024,1024]{1,0:T(8,128)}), f32[32,1024]{1,0:T(8,128)}) %reduce-scatter.10.cloned.1.call-update) | async-done | bytes 131088 | tf_op jit(solution)/shard_map/reduce_scatter | solution.py:345
  1778.3 139.9 %reduce-scatter.16.cloned.1.call-done = f32[1024,32]{0,1:T(8,128)} async-done(((f32[1024,1024]{0,1:T(8,128)}), f32[1024,32]{0,1:T(8,128)}) %reduce-scatter.16.cloned.1.call-update) | async-done | bytes 131088 | tf_op jit(solution)/shard_map/reduce_scatter | solution.py:348
  1918.1 362.7 %reduce-scatter.20.cloned.1.call-done = f32[16,32,512]{2,1,0:T(8,128)} async-done(((f32[16,1024,512]{2,1,0:T(8,128)}), f32[16,32,512]{2,1,0:T(8,128)}) %reduce-scatter.20.cloned.1.call-update) | async-done | bytes 1048592 | tf_op jit(solution)/shard_map/reduce_scatter | solution.py:253
  2280.9 709.0 %reduce-scatter.18.cloned.1.call-done = f32[16,32,1024]{2,1,0:T(8,128)} async-done(((f32[16,1024,1024]{2,1,0:T(8,128)}), f32[16,32,1024]{2,1,0:T(8,128)}) %reduce-scatter.18.cloned.1.call-update) | async-done | bytes 2097168 | tf_op jit(solution)/shard_map/reduce_scatter | solution.py:252
  (249 shorter events, 34.7 us)
Async XLA Ops:
  7.2 744.3 %all-gather.11.cloned.1.call-start = ((), (), s32[]{:S(2)}) async-start(), calls=%async_computation.8 | async-start | bytes 1572864 | tf_op jit(solution)/shard_map/all_gather | solution.py:166
  7.9 751.3 %all-gather.9.cloned.1.call-start = ((), (), s32[]{:S(2)}) async-start(), calls=%async_computation.7 | async-start | bytes 1572864 | tf_op jit(solution)/shard_map/all_gather | solution.py:167
  8.7 754.2 %all-gather.13.cloned.1.call-start = ((), (), s32[]{:S(2)}) async-start(), calls=%async_computation.9 | async-start | bytes 3145728 | tf_op jit(solution)/shard_map/all_gather | solution.py:165
  9.4 812.0 %all-gather.15.cloned.1.call-start = ((), (), s32[]{:S(2)}) async-start(), calls=%async_computation.10 | async-start | bytes 3145728 | tf_op jit(solution)/shard_map/all_gather | solution.py:168
  10.0 985.7 %all-gather.17.cloned.1.call-start = ((), (), s32[]{:S(2)}) async-start(), calls=%async_computation.11 | async-start | bytes 25165824 | tf_op jit(solution)/shard_map/all_gather | solution.py:220
  10.6 627.8 %copy-start.69 = (bf16[512]{0:T(512)(128)(2,1)S(1)}, bf16[512]{0:T(512)(128)(2,1)}, u32[]{:S(2)}) copy-start(bf16[512]{0:T(512)(128)(2,1)} %param.19) | copy-start | bytes 3076
  10.6 632.7 %copy-start.38 = (s32[1,512,8]{1,2,0:T(8,128)S(1)}, s32[1,512,8]{1,2,0:T(8,128)}, u32[]{:S(2)}) copy-start(s32[1,512,8]{1,2,0:T(8,128)} %param.23) | copy-start | bytes 49156
  10.6 681.7 %copy-start.18 = (bf16[1,512,1024]{2,1,0:T(8,128)(2,1)S(1)}, bf16[1,512,1024]{2,1,0:T(8,128)(2,1)}, u32[]{:S(2)}) copy-start(bf16[1,512,1024]{2,1,0:T(8,128)(2,1)} %param.25) | copy-start | bytes 3145732
  10.6 1075.6 %all-gather.19.cloned.1.call-start = ((), (), s32[]{:S(2)}) async-start(), calls=%async_computation.12 | async-start | bytes 50331648 | tf_op jit(solution)/shard_map/all_gather | solution.py:245
  11.2 1354.7 %reduce-scatter.22.cloned.1.call-start = ((), (), s32[]{:S(2)}) async-start(), calls=%async_computation.19 | async-start | bytes 540672
  11.2 911.0 %collective-permute-start.2 = (bf16[1,8,1024,1024]{3,2,1,0:T(8,128)(2,1)}, bf16[1,8,1024,1024]{3,2,1,0:T(8,128)(2,1)}, u32[]{:S(2)}, u32[]{:S(2)}) collective-permute-start(bf16[1,8,1024,1024]{3,2,1,0:T(8,128)(2,1)} %bitcast.201), channel_id=1, source_target_pairs={{0,16},{16,0},{1,17},{17,1},{2,18},{18,2},{3,19},{19,3},{4,20},{20... | collective-permute-start | bytes 50331656 | tf_op jit(solution)/shard_map/ppermute | solution.py:36
  637.7 129.1 %copy-start.52 = (f32[2,1,512]{2,1,0:T(1,128)}, f32[2,1,512]{2,1,0:T(1,128)S(1)}, u32[]{:S(2)}) copy-start(f32[2,1,512]{2,1,0:T(1,128)S(1)} %convert_element_type.171) | copy-start | bytes 12292
  643.4 48.9 %copy-start.13 = (s32[1,512,8]{2,1,0:T(8,128)}, s32[1,512,8]{2,1,0:T(8,128)S(1)}, u32[]{:S(2)}) copy-start(s32[1,512,8]{2,1,0:T(8,128)S(1)} %copy.78) | copy-start | bytes 49156
  647.5 101.5 %copy-start.55 = (s32[4096,1]{0,1:T(1,128)}, s32[4096,1]{0,1:T(1,128)S(1)}, u32[]{:S(2)}) copy-start(s32[4096,1]{0,1:T(1,128)S(1)} %compare_select_fusion.1) | copy-start | bytes 49156
  692.5 27.3 copy-start
  719.8 24.8 copy-start.66
  719.8 28.9 copy-start.5
  748.6 104.6 %copy-start.47 = (bf16[1024,16]{0,1:T(8,128)(2,1)}, bf16[1024,16]{0,1:T(8,128)(2,1)S(1)}, u32[]{:S(2)}) copy-start(bf16[1024,16]{0,1:T(8,128)(2,1)S(1)} %all_gather.34) | copy-start | bytes 98308
  749.0 17.8 copy-start.58
  749.9 19.9 copy-start.30
  749.9 19.9 copy-start.32
  754.0 25.7 copy-start.21
  754.0 25.7 copy-start.23
  755.0 24.7 collective-permute-start.1
  761.3 46.1 %copy-start.40 = (bf16[512,512]{0,1:T(8,128)(2,1)}, bf16[512,512]{0,1:T(8,128)(2,1)S(1)}, u32[]{:S(2)}) copy-start(bf16[512,512]{0,1:T(8,128)(2,1)S(1)} %convolution_convert_fusion.1) | copy-start | bytes 1572868
  761.3 46.1 %collective-permute-start = (bf16[512,8,64]{0,2,1:T(8,128)(2,1)S(1)}, bf16[512,8,64]{0,2,1:T(8,128)(2,1)S(1)}, u32[]{:S(2)}, u32[]{:S(2)}) collective-permute-start(bf16[512,8,64]{0,2,1:T(8,128)(2,1)S(1)} %bitcast.229), channel_id=1, source_target_pairs={{0,16},{1,17},{2,18},{3,19},{4,20},{5,21},{6,22},{7,23},{8,24},{9,... | collective-permute-start | bytes 1572872 | tf_op jit(solution)/shard_map/ppermute | solution.py:48
  766.8 12.9 copy-start.44
  770.2 24.0 copy-start.25
  770.2 24.0 copy-start.27
  807.4 14.0 copy-start.42
  824.7 28.4 copy-start.64
  824.7 28.4 copy-start.60
  826.3 26.9 copy-start.2
  826.3 27.3 copy-start.4
  853.6 33.2 %copy-start.14 = (s32[1,512,8]{2,1,0:T(8,128)S(1)}, s32[1,512,8]{2,1,0:T(8,128)}, u32[]{:S(2)}) copy-start(s32[1,512,8]{2,1,0:T(8,128)} %copy-done.13) | copy-start | bytes 49156
  853.6 34.2 %copy-start.54 = (s32[4096]{0:T(1024)S(1)}, s32[4096]{0:T(1024)}, u32[]{:S(2)}) copy-start(s32[4096]{0:T(1024)} %squeeze.32) | copy-start | bytes 49156
  903.5 92.1 %copy-start.49 = (f32[16,384]{1,0:T(8,128)}, f32[16,384]{1,0:T(8,128)S(1)}, u32[]{:S(2)}) copy-start(f32[16,384]{1,0:T(8,128)S(1)} %mul.437) | copy-start | bytes 73732
  944.8 22.7 copy-start.45
  1026.0 18.3 copy-start.51
  1044.3 30.6 %copy-start.1 = (f32[512,1024]{1,0:T(8,128)S(1)}, f32[512,1024]{1,0:T(8,128)}, u32[]{:S(2)}) copy-start(f32[512,1024]{1,0:T(8,128)} %copy-done) | copy-start | bytes 6291460
  1044.3 30.6 %copy-start.17 = (f32[512,8]{1,0:T(8,128)S(1)}, f32[512,8]{1,0:T(8,128)}, u32[]{:S(2)}) copy-start(f32[512,8]{1,0:T(8,128)} %fusion.61) | copy-start | bytes 49156
  1075.0 11.2 copy-start.39
  1143.1 8.2 copy-start.57
  1143.1 8.2 copy-start.61
  1180.1 27.9 copy-start.26
  1180.1 27.9 copy-start.28
  1208.0 15.8 copy-start.3
  1220.3 14.1 copy-start.31
  1220.3 14.1 copy-start.33
  1220.3 15.1 copy-start.6
  1220.3 15.2 copy-start.53
  1220.3 15.1 copy-start.59
  1222.5 10.3 collective-permute-start.3
  1225.9 276.3 %reduce-scatter.12.cloned.1.call-start = ((), (), s32[]{:S(2)}) async-start(), calls=%async_computation.14 | async-start | bytes 2162688 | tf_op jit(solution)/shard_map/reduce_scatter | solution.py:346
  1237.8 400.2 %reduce-scatter.14.cloned.1.call-start = ((), (), s32[]{:S(2)}) async-start(), calls=%async_computation.15 | async-start | bytes 2162688 | tf_op jit(solution)/shard_map/reduce_scatter | solution.py:347
  1253.8 14.5 copy-start.22
  1253.8 14.5 copy-start.24
  1253.8 10.5 collective-permute-start.4
  1267.9 510.3 %reduce-scatter.10.cloned.1.call-start = ((), (), s32[]{:S(2)}) async-start(), calls=%async_computation.13 | async-start | bytes 4325376 | tf_op jit(solution)/shard_map/reduce_scatter | solution.py:345
  1282.1 636.1 %reduce-scatter.16.cloned.1.call-start = ((), (), s32[]{:S(2)}) async-start(), calls=%async_computation.16 | async-start | bytes 4325376 | tf_op jit(solution)/shard_map/reduce_scatter | solution.py:348
  1288.2 992.7 %reduce-scatter.20.cloned.1.call-start = ((), (), s32[]{:S(2)}) async-start(), calls=%async_computation.18 | async-start | bytes 34603008 | tf_op jit(solution)/shard_map/reduce_scatter | solution.py:253
  1313.6 1676.3 %reduce-scatter.18.cloned.1.call-start = ((), (), s32[]{:S(2)}) async-start(), calls=%async_computation.17 | async-start | bytes 69206016 | tf_op jit(solution)/shard_map/reduce_scatter | solution.py:252
  1347.9 19.4 copy-start.36
  1371.5 46.1 %copy-start.63 = (f32[512]{0:T(512)S(1)}, f32[512]{0:T(512)}, u32[]{:S(2)}) copy-start(f32[512]{0:T(512)} %copy-done.62) | copy-start | bytes 6148
  (24 other events, 64.3 us)
Sparse Core Ops, SparseCore 0:
  9.6 34.9 all-gather.10
  46.1 32.6 all-gather.8
  80.3 55.6 all-gather.12
  137.5 55.6 all-gather.14
  194.6 378.7 all-gather.16
  574.8 428.4 all-gather.18
  1226.0 139.8 reduce-scatter.21
  1368.8 133.2 reduce-scatter.11
  1505.0 132.9 reduce-scatter.13
  1640.8 137.4 reduce-scatter.9
  1781.2 136.8 reduce-scatter.15
  1921.0 359.8 reduce-scatter.19
  2283.9 705.8 reduce-scatter.17
